TPU v7x, 32 devices: a whole 2x2x4 slice. The times are simulated.
32 devices in a mesh: grp: 2 (over x), wide: 16 (over z, y, core).
Axes of the slice: x: 2, y: 2, z: 4, core: 2. Of those that a mesh axis runs over, the one named last changes fastest.
Arguments:
- hidden: bfloat16 [32, 256, 8192], P(('grp', 'wide')), parts along dimension 0, may hold values from -6 to 6
- output_gradient: bfloat16 [32, 256, 8192], P(('grp', 'wide')), parts along dimension 0, may hold values from -6 to 6
- adapter_up_factor: bfloat16 [8192, 64], replicated, may hold values from -0.0625 to 0.0625
- first_moment_estimate: float32 [64, 8192], P(None, 'wide'), may hold values from -0.06 to 0.06
- second_moment_estimate: float32 [64, 8192], P(None, 'wide'), may hold values from 0.0001 to 0.01
- lengths: int32 [32], P(('grp', 'wide')), parts along dimension 0, may hold values from 32 to 256, as said below
- seeds: int32 [128], P('wide'), may hold values from 0 to 16777215
Outputs:
- features: float32 [32, 4096], P(('grp', 'wide')), parts along dimension 0
There are 2 independent parts, one for each index of `grp`. A program takes and returns all parts, laid end to end along the dimension named above; an argument that names none is the same for every part. Nothing has to cross between parts.
Inputs may be any that keep to these rules, and one draw needn't show every extreme that they name: `lengths`: some sequence has exactly 256 live tokens and some has 32.
All inputs are finite; a program needn't handle non-finite values.
Results may differ from a plain program's by a relative error of at most 0.0039.
Values may be sent and summed in bfloat16 or wider, within the bound.
No kernel may reach another device: no remote copies, remote signals or barrier semaphores. Data moves between devices by JAX's collectives and lax.ppermute only.
A program may use at most 384 MiB of HBM per device.

v0:
```python
import jax
import jax.numpy as jnp
from jax import lax
from jax.sharding import PartitionSpec as P

K = 4096
CB = 64
RB = 8


def mix_bits(hashed):
    for turn in range(2):
        hashed = hashed & 2147483647
        hashed = hashed ^ jnp.right_shift(hashed, 16)
        hashed = hashed * 73244475
    hashed = hashed & 2147483647
    hashed = hashed ^ jnp.right_shift(hashed, 16)
    return hashed


def build_signs(rank_rows, own_cols, seeds):
    col_blocks = own_cols // CB
    row_groups = rank_rows // RB
    row_ids = lax.broadcasted_iota(jnp.int32, (RB, CB, K), 0)
    col_ids = lax.broadcasted_iota(jnp.int32, (RB, CB, K), 1)
    feat_ids = lax.broadcasted_iota(jnp.int32, (RB, CB, K), 2)

    def fill_step(loop_index, table):
        loop_index = loop_index.astype(jnp.int32)
        col_pos = loop_index // row_groups
        grp_pos = loop_index % row_groups
        param_ids = (grp_pos * RB + row_ids) * CB + col_ids
        hashed = mix_bits(param_ids * 1000003 + feat_ids * 7919 + seeds[col_pos])
        block = (1 - 2 * (hashed & 1)).astype(jnp.bfloat16)
        return lax.dynamic_update_slice(table, block, (grp_pos * RB, col_pos * CB, jnp.int32(0)))

    table = jnp.zeros((rank_rows, own_cols, K), jnp.bfloat16)
    table = lax.fori_loop(0, col_blocks * row_groups, fill_step, table)
    return table.reshape(rank_rows * own_cols, K)


def shards(
    hidden,
    output_gradient,
    adapter_up_factor,
    first_moment_estimate,
    second_moment_estimate,
    lengths,
    seeds,
):
    own_seqs, tok_slots = (hidden.shape[0], hidden.shape[1])
    rank_reduced = jnp.einsum(
        "nuk,kv->nuv", output_gradient, adapter_up_factor, preferred_element_type=jnp.float32
    )
    live_mask = lax.broadcasted_iota(jnp.int32, (own_seqs, tok_slots), 1) < lengths[:, None]
    rank_reduced = jnp.where(live_mask[:, :, None], rank_reduced, 0.0).astype(jnp.bfloat16)
    summed = jnp.einsum("str,std->srd", rank_reduced, hidden, preferred_element_type=jnp.float32)
    seq_grad = (summed / lengths.astype(jnp.float32)[:, None, None]).astype(jnp.bfloat16)
    regrouped = lax.all_to_all(seq_grad, "wide", split_axis=2, concat_axis=0, tiled=True)
    grad_full = regrouped.astype(jnp.float32)
    first_new = 0.9 * first_moment_estimate[None] + 0.1 * grad_full
    second_new = 0.999 * second_moment_estimate[None] + 0.001 * grad_full * grad_full
    update = (first_new / (jnp.sqrt(second_new) + 1e-08)).astype(jnp.bfloat16)
    all_seqs, rank_rows, own_cols = update.shape
    flat_update = update.reshape(all_seqs, rank_rows * own_cols)
    signs = build_signs(rank_rows, own_cols, seeds)
    partial_value = jnp.dot(flat_update, signs, preferred_element_type=jnp.float32)
    totals = lax.psum(partial_value, "wide")
    own_rows = lax.dynamic_slice_in_dim(totals, lax.axis_index("wide") * own_seqs, own_seqs, 0)
    return own_rows * lax.rsqrt(jnp.mean(own_rows * own_rows, axis=1, keepdims=True) + 1e-06)


def solution(mesh):
    placed = (
        P(("grp", "wide"), None, None),
        P(("grp", "wide"), None, None),
        P(),
        P(None, "wide"),
        P(None, "wide"),
        P(("grp", "wide")),
        P("wide"),
    )
    return jax.shard_map(
        shards, mesh=mesh, in_specs=placed, out_specs=P(("grp", "wide"), None), check_vma=False
    )
```

profile of v0, /device:TPU:0, one launch (start us, length us, event | category | flops | bytes accessed | tf_op | source)
XLA Modules:
  0.0 859.6 jit_solution(11713822607061688417)
XLA Ops:
  21.7 45.2 %reduce.1 = bf16[8192,64]{1,0:T(8,128)(2,1)S(1)} reduce(bf16[8192,1,64]{2,1,0:T(2,128)(2,1)} %bitcast.44, bf16[]{:T(256)} %broadcast.116), dimensions={1}, to_apply=%bitcast.32.reduce_sub_computation | reduce | bytes 2097154
  69.1 7.4 all-to-all-start
  76.8 81.1 %broadcast_in_dim.23 = bf16[64,512,4096]{2,1,0:T(8,128)(2,1)} broadcast(bf16[]{:T(256)} %constant.173.clone.1), dimensions={} | broadcast | bytes 268435456 | tf_op jit(solution)/shard_map/broadcast_in_dim | solution.py:37
  157.9 496.9 %while.16 = (s32[]{:T(128)}, bf16[64,512,4096]{2,1,0:T(8,128)(2,1)}, s32[8]{0:T(128)S(1)}, s32[]{:T(128)}, s32[]{:T(128)}, /*index=5*/s32[]{:T(128)}, s32[]{:T(1...) while((s32[]{:T(128)}, bf16[64,512,4096]{2,1,0:T(8,128)(2,1)}, s32[8]{0:T(128)S(1)}, ...), condition=%wide.region_1.2_spmd.clone, body=%wide.region_0.1_spmd.clone.sunk | while | flops 46137368 | bytes 4195198 | solution.py:38
  158.5 7.2 fusion.57
  174.1 7.2 fusion.57
  181.9 7.2 fusion.57
  189.7 7.2 fusion.57
  205.2 7.2 fusion.57
  220.8 7.2 fusion.57
  236.3 7.2 fusion.57
  251.8 7.2 fusion.57
  267.4 7.2 fusion.57
  414.7 7.2 fusion.57
  430.2 7.2 fusion.57
  445.8 7.2 fusion.57
  476.9 7.2 fusion.57
  507.9 7.2 fusion.57
  601.0 7.2 fusion.57
  624.2 7.2 fusion.57
  639.8 7.2 fusion.57
  661.8 8.5 bitcast_convert_fusion
  673.6 84.2 %convolution_bitcast_fusion = f32[16,4096]{1,0:T(8,128)} fusion(bf16[64,512,4096]{2,1,0:T(8,128)(2,1)} %get-tuple-element.162, f32[1,64,16,512]{3,2,1,0:T(8,128)S(1)} %copy.9, f32[64,512]{1,0:T(8,128)S(1)} %get-tuple-element.179, f32[64,512]{1,0:T(8,128)S(1)} %get-tuple-element.180), kind=kOutput, calls=%fused_computation.26 | convolution fusion | flops 4299161600 | bytes 271056896 | tf_op jit(solution)/shard_map/dot_general | solution.py:67
  757.8 91.2 %all-reduce.2.cloned.1.call-done = f32[16,4096]{1,0:T(8,128)} async-done(((f32[16,4096]{1,0:T(8,128)}), f32[16,4096]{1,0:T(8,128)}) %all-reduce.2.cloned.1.call-update) | async-done | bytes 262160 | tf_op jit(solution)/shard_map/psum | solution.py:68
  (132 shorter events, 404.9 us)
Async XLA Ops:
  6.5 1.2 copy-start
  69.1 585.7 %all-to-all-start = ((bf16[16,2,16384]{2,1,0:T(2,128)(2,1)}), bf16[16,2,16384]{2,1,0:T(2,128)(2,1)S(1)}, u32[]{:S(2)}, u32[]{:S(2)}) async-start(bf16[16,2,16384]{2,1,0:T(2,128)(2,1)} %reshape.53), calls=%async_computation | async-start | bytes 2097152 | tf_op jit(solution)/shard_map/all_to_all | solution.py:59
  76.5 772.5 %all-reduce.2.cloned.1.call-start = ((), (), s32[]{:S(2)}) async-start(), calls=%async_computation.1 | async-start | bytes 524288 | tf_op jit(solution)/shard_map/psum | solution.py:68
  76.8 81.1 %copy-start.3 = (s32[8]{0:T(128)S(1)}, s32[8]{0:T(128)}, u32[]{:S(2)}) copy-start(s32[8]{0:T(128)} %param.15) | copy-start | bytes 100
  157.9 496.9 %copy-start.1 = (f32[64,512]{1,0:T(8,128)S(1)}, f32[64,512]{1,0:T(8,128)}, u32[]{:S(2)}) copy-start(f32[64,512]{1,0:T(8,128)} %param.13) | copy-start | bytes 393220
  157.9 496.9 %copy-start.2 = (f32[64,512]{1,0:T(8,128)S(1)}, f32[64,512]{1,0:T(8,128)}, u32[]{:S(2)}) copy-start(f32[64,512]{1,0:T(8,128)} %param.12) | copy-start | bytes 393220
Sparse Core Ops, SparseCore 0:
  758.0 91.0 all-reduce.1
where the time goes:
time: 861 us; the launch traced here: 860 us
  other arithmetic  515 us (60%)
  local copies, waits for them, and re-layouts  140 us (16%)
  waiting for transfers between devices  91.2 us (11%)
  matrix products  90.7 us (11%)
  between operations  14.9 us (2%)
    dynamic_update_slice x64, other arithmetic, fill_step(): lax.dynamic_update_slice(table, block, (grp_pos * RB, col_pos * CB, jnp.i...  459 us
    psum x1, waiting for transfers between devices, shards(): totals = lax.psum(partial_value, 'wide')  91.2 us
    dot_general x1, matrix products, shards(): jnp.dot(flat_update, signs, preferred_element_type=jnp.float32)  84.2 us
    broadcast_in_dim x1, local copies, waits for them, and re-layouts, build_signs(): table = jnp.zeros((rank_rows, own_cols, K), jnp.bfloat16)  81.1 us
    unnamed x1, other arithmetic  45.2 us
    dynamic_slice x64, local copies, waits for them, and re-layouts, fill_step(): hashed = mix_bits(param_ids * 1000003 + feat_ids * 7919 + seeds[col_pos])  38.1 us
  transfers between devices with their start and end apart: 2, of which 1 were waited for; matrix products, arithmetic and copies ran while one was open for 67% of the time, Pallas kernels for 0%

commit v1 on v0

--- a/solution.py
+++ b/solution.py
@@ -65,7 +65,8 @@
     flat_update = update.reshape(all_seqs, rank_rows * own_cols)
     signs = build_signs(rank_rows, own_cols, seeds)
     partial_value = jnp.dot(flat_update, signs, preferred_element_type=jnp.float32)
-    totals = lax.psum(partial_value, "wide")
+    parts = lax.all_gather(partial_value, "wide", axis=0, tiled=False)
+    totals = parts.sum(axis=0)
     own_rows = lax.dynamic_slice_in_dim(totals, lax.axis_index("wide") * own_seqs, own_seqs, 0)
     return own_rows * lax.rsqrt(jnp.mean(own_rows * own_rows, axis=1, keepdims=True) + 1e-06)
 

time: 861 us -> 822 us (0.955)
  waiting for transfers between devices: 91.2 us -> 51.9 us
    psum x1 -> x0, waiting for transfers between devices: 91.2 us -> none  [shards(): totals = lax.psum(partial_value, 'wide')]
    all_gather x0 -> x1, waiting for transfers between devices: none -> 51.8 us  [shards(): parts = lax.all_gather(partial_value, 'wide', axis=0, tiled=False)]
  transfers between devices with their start and end apart: 2 -> 2, of which waited for: 1 -> 1; matrix products, arithmetic and copies ran while one was open for 67% -> 70% of each run, Pallas kernels for 0% -> 0%
where the time goes in v1:
time: 822 us; the launch traced here: 821 us
  other arithmetic  516 us (63%)
  local copies, waits for them, and re-layouts  140 us (17%)
  matrix products  90.7 us (11%)
  waiting for transfers between devices  51.9 us (6%)
  between operations  14.9 us (2%)
    dynamic_update_slice x64, other arithmetic, fill_step(): lax.dynamic_update_slice(table, block, (grp_pos * RB, col_pos * CB, jnp.i...  459 us
    dot_general x1, matrix products, shards(): jnp.dot(flat_update, signs, preferred_element_type=jnp.float32)  84.2 us
    broadcast_in_dim x1, local copies, waits for them, and re-layouts, build_signs(): table = jnp.zeros((rank_rows, own_cols, K), jnp.bfloat16)  81.1 us
    all_gather x1, waiting for transfers between devices, shards(): parts = lax.all_gather(partial_value, 'wide', axis=0, tiled=False)  51.8 us
    unnamed x1, other arithmetic  45.2 us
    dynamic_slice x64, local copies, waits for them, and re-layouts, fill_step(): hashed = mix_bits(param_ids * 1000003 + feat_ids * 7919 + seeds[col_pos])  38.1 us
  transfers between devices with their start and end apart: 2, of which 1 were waited for; matrix products, arithmetic and copies ran while one was open for 70% of the time, Pallas kernels for 0%

profile of v1, /device:TPU:0, one launch (start us, length us, event | category | flops | bytes accessed | tf_op | source)
XLA Modules:
  0.0 820.9 jit_solution(4725096752795277773)
XLA Ops:
  21.7 45.2 %reduce.1 = bf16[8192,64]{1,0:T(8,128)(2,1)S(1)} reduce(bf16[8192,1,64]{2,1,0:T(2,128)(2,1)} %bitcast.45, bf16[]{:T(256)} %broadcast.116), dimensions={1}, to_apply=%bitcast.33.reduce_sub_computation | reduce | bytes 2097154
  69.1 7.4 all-to-all-start
  76.8 81.1 %broadcast_in_dim.23 = bf16[64,512,4096]{2,1,0:T(8,128)(2,1)} broadcast(bf16[]{:T(256)} %constant.173.clone.1), dimensions={} | broadcast | bytes 268435456 | tf_op jit(solution)/shard_map/broadcast_in_dim | solution.py:37
  157.9 496.9 %while.16 = (s32[]{:T(128)}, bf16[64,512,4096]{2,1,0:T(8,128)(2,1)}, s32[8]{0:T(128)S(1)}, s32[]{:T(128)}, s32[]{:T(128)}, /*index=5*/s32[]{:T(128)}, s32[]{:T(1...) while((s32[]{:T(128)}, bf16[64,512,4096]{2,1,0:T(8,128)(2,1)}, s32[8]{0:T(128)S(1)}, ...), condition=%wide.region_1.2_spmd.clone, body=%wide.region_0.1_spmd.clone.sunk | while | flops 46137368 | bytes 4195198 | solution.py:38
  158.5 7.2 fusion.57
  174.1 7.2 fusion.57
  181.9 7.2 fusion.57
  189.7 7.2 fusion.57
  205.2 7.2 fusion.57
  220.8 7.2 fusion.57
  236.3 7.2 fusion.57
  251.8 7.2 fusion.57
  267.4 7.2 fusion.57
  414.7 7.2 fusion.57
  430.2 7.2 fusion.57
  445.8 7.2 fusion.57
  476.9 7.2 fusion.57
  507.9 7.2 fusion.57
  601.0 7.2 fusion.57
  624.2 7.2 fusion.57
  639.8 7.2 fusion.57
  661.8 8.5 %bitcast_convert_fusion = f32[1,64,8192]{1,0,2:T(1,128)} fusion(bf16[8192,1,64]{2,1,0:T(2,128)(2,1)} %reshape.55), kind=kLoop, calls=%fused_computation.56 | loop fusion | flops 524288 | bytes 3145728 | tf_op jit(solution)/shard_map/convert_element_type | solution.py:60
  673.6 84.2 %convolution_bitcast_fusion = f32[16,4096]{1,0:T(8,128)} fusion(bf16[64,512,4096]{2,1,0:T(8,128)(2,1)} %get-tuple-element.162, f32[1,64,16,512]{3,2,1,0:T(8,128)S(1)} %copy.9, f32[64,512]{1,0:T(8,128)S(1)} %get-tuple-element.179, f32[64,512]{1,0:T(8,128)S(1)} %get-tuple-element.180), kind=kOutput, calls=%fused_computation.26 | convolution fusion | flops 4299161600 | bytes 271056896 | tf_op jit(solution)/shard_map/dot_general | solution.py:67
  757.8 51.8 %all-gather.3.cloned.1.call-done = f32[256,4096]{1,0:T(8,128)} async-done(((f32[16,4096]{1,0:T(8,128)}), f32[256,4096]{1,0:T(8,128)}) %all-gather.3.cloned.1.call-update) | async-done | bytes 4194320 | tf_op jit(solution)/shard_map/all_gather | solution.py:68
  (133 shorter events, 405.5 us)
Async XLA Ops:
  6.5 1.2 copy-start
  69.1 585.7 %all-to-all-start = ((bf16[16,2,16384]{2,1,0:T(2,128)(2,1)}), bf16[16,2,16384]{2,1,0:T(2,128)(2,1)S(1)}, u32[]{:S(2)}, u32[]{:S(2)}) async-start(bf16[16,2,16384]{2,1,0:T(2,128)(2,1)} %reshape.54), calls=%async_computation | async-start | bytes 2097152 | tf_op jit(solution)/shard_map/all_to_all | solution.py:59
  76.5 733.1 %all-gather.3.cloned.1.call-start = ((), (), s32[]{:S(2)}) async-start(), calls=%async_computation.1 | async-start | bytes 4456448 | tf_op jit(solution)/shard_map/all_gather | solution.py:68
  76.8 81.1 %copy-start.3 = (s32[8]{0:T(128)S(1)}, s32[8]{0:T(128)}, u32[]{:S(2)}) copy-start(s32[8]{0:T(128)} %param.15) | copy-start | bytes 100
  157.9 496.9 %copy-start.1 = (f32[64,512]{1,0:T(8,128)S(1)}, f32[64,512]{1,0:T(8,128)}, u32[]{:S(2)}) copy-start(f32[64,512]{1,0:T(8,128)} %param.13) | copy-start | bytes 393220
  157.9 496.9 %copy-start.2 = (f32[64,512]{1,0:T(8,128)S(1)}, f32[64,512]{1,0:T(8,128)}, u32[]{:S(2)}) copy-start(f32[64,512]{1,0:T(8,128)} %param.12) | copy-start | bytes 393220
Sparse Core Ops, SparseCore 0:
  757.9 51.6 all-gather.2
